TPU v7x, 32 devices: a whole 2x2x4 slice. The times are simulated.
32 devices in a mesh: grp: 2 (over x), tile: 8 (over z, y), wave: 2 (over core).
Axes of the slice: x: 2, y: 2, z: 4, core: 2. Of those that a mesh axis runs over, the one named last changes fastest.
Arguments:
- residual: float32 [16, 8, 2, 8, 128], P(('grp', 'tile'), 'wave'), parts along dimension 0, may hold values from -210 to 210
- kernel: bfloat16 [16, 8, 9, 2, 128, 128], P(('grp', 'tile'), 'wave'), parts along dimension 0, may hold values from -0.125 to 0.125
- offsets: float32 [16, 8, 2, 128], P(('grp', 'tile'), 'wave'), parts along dimension 0, may hold values from 0 to 1
- neighbor: int32 [16, 8, 9], P(('grp', 'tile'), 'wave'), parts along dimension 0, may hold values from 0 to 8, each once within a row
- frequency: int32 [16], P('grp'), parts along dimension 0, may hold values from 0 to 7, each once
- lattice_x: int32 [128], replicated, may hold values from 0 to 127, each once
- lattice_y: int32 [128], replicated, may hold values from 0 to 127, each once
- spectral_weight: float32 [8, 128, 128], replicated, may hold values from 0.1 to 3
Outputs:
- image_two: float32 [16, 8, 2, 8, 128], P(('grp', 'tile'), 'wave'), parts along dimension 0
- arnoldi: float32 [8, 8], P('grp'), parts along dimension 0
There are 2 independent parts, one for each index of `grp`. A program takes and returns all parts, laid end to end along the dimension named above; an argument that names none is the same for every part. Nothing has to cross between parts.
Inputs may be any that keep to these rules, and one draw needn't show every extreme that they name: `neighbor`: each row names each of the nine neighbour slots once. `frequency`: each index appears once. `lattice_x`: each index appears once. `lattice_y`: each index appears once.
All inputs are finite; a program needn't handle non-finite values.
Results may differ from a plain program's by a relative error of at most 0.013.
Values may be sent and summed in bfloat16 or wider, within the bound.
A program may use at most 64 MiB of HBM per device.

v0:
```python
import math
import jax
import jax.numpy as jnp
from jax import lax
from jax.sharding import PartitionSpec as P

two_pi = 2.0 * math.pi
eps_norm = 1e-06


def padded_2(array, sides, width):
    for axis, dim in sides:
        size, length = (lax.axis_size(axis), array.shape[dim])
        up = [(i, (i + 1) % size) for i in range(size)]
        down = [(j, i) for i, j in up]
        last = lax.slice_in_dim(array, length - width, length, axis=dim)
        initial = lax.slice_in_dim(array, 0, width, axis=dim)
        before = lax.ppermute(last, axis, up)
        after = lax.ppermute(initial, axis, down)
        array = jnp.concatenate([before, array, after], axis=dim)
    return array


def phase_table(position, harmonic):
    phase_angle = two_pi * (position[:, None] * harmonic[None, :])
    return (jnp.cos(phase_angle).astype(jnp.bfloat16), jnp.sin(phase_angle).astype(jnp.bfloat16))


def project_rows(cosine_cols, sine_cols, twisted):
    row_count = cosine_cols.shape[1]
    stacked = jnp.concatenate([cosine_cols, sine_cols], 1)
    gram_matrix = lax.dot_general(
        stacked, twisted, (((0,), (0,)), ((), ())), preferred_element_type=jnp.float32
    )
    gram_matrix = gram_matrix.reshape(2, row_count, 2, -1)
    coef_real = gram_matrix[0, :, 0] + gram_matrix[1, :, 1]
    coef_imag = gram_matrix[0, :, 1] - gram_matrix[1, :, 0]
    return jnp.stack([coef_real, coef_imag], 1)


def expand_rows(cosine_cols, sine_cols, scaled):
    row_count = scaled.shape[0]
    upper_rows = scaled.reshape(row_count, -1)
    lower_rows = jnp.stack([-scaled[:, 1], scaled[:, 0]], 1).reshape(row_count, -1)
    matrix = jnp.concatenate([upper_rows, lower_rows], 0)
    stacked = jnp.concatenate([cosine_cols, sine_cols], 1)
    return jnp.dot(stacked, matrix, preferred_element_type=jnp.float32)


def twist_density(panel_density, cosine_y, sine_y):
    density_real = panel_density[:, 0, :, None].astype(jnp.float32)
    density_imag = panel_density[:, 1, :, None].astype(jnp.float32)
    wave_cos = cosine_y.astype(jnp.float32)[:, None, :]
    wave_sin = sine_y.astype(jnp.float32)[:, None, :]
    part_real = wave_cos * density_real + wave_sin * density_imag
    part_imag = wave_cos * density_imag - wave_sin * density_real
    return (
        jnp.stack([part_real, part_imag], 1)
        .reshape(panel_density.shape[0], -1)
        .astype(jnp.bfloat16)
    )


def finish(summed, cosine_y, sine_y, vectors):
    shaped = summed.reshape(summed.shape[0], 2, vectors, -1)
    wave_cos = cosine_y.astype(jnp.float32)[:, None, :]
    wave_sin = sine_y.astype(jnp.float32)[:, None, :]
    far_real = jnp.sum(shaped[:, 0] * wave_cos - shaped[:, 1] * wave_sin, -1)
    far_imag = jnp.sum(shaped[:, 0] * wave_sin + shaped[:, 1] * wave_cos, -1)
    return jnp.stack([far_real, far_imag], 1)


def combine_near(product, vectors):
    first_half = product[:, 0]
    second = product[:, 1]
    near_real = first_half[:, :vectors] - second[:, vectors:]
    near_imag = second[:, :vectors] + first_half[:, vectors:]
    return jnp.stack([near_real, near_imag], 1)


def panel_sum(values):
    return jnp.sum(values, axis=(0, 1, 3))


def per_device(
    residual, kernel, offsets, neighbor, frequency, lattice_x, lattice_y, spectral_weight
):
    strips = residual.shape[0]
    tiles_y = residual.shape[1]
    vectors = residual.shape[3]
    panels_t = residual.shape[4]
    modes_x = spectral_weight.shape[1]
    modes_y = spectral_weight.shape[2]
    count_x = lax.axis_size("tile") * strips
    count_y = lax.axis_size("wave") * tiles_y
    devices = lax.axis_size("tile") * lax.axis_size("wave")
    panels = count_x * count_y * panels_t
    local_rows = strips * tiles_y * panels_t
    column = (lax.axis_index("tile") * strips + jnp.arange(strips)).astype(jnp.float32)
    row_index = (lax.axis_index("wave") * tiles_y + jnp.arange(tiles_y)).astype(jnp.float32)
    position_x = ((column[:, None, None] + offsets[:, :, 0, :]) / count_x).reshape(-1)
    position_y = ((row_index[None, :, None] + offsets[:, :, 1, :]) / count_y).reshape(-1)
    harmonic_x = (lattice_x - modes_x // 2).astype(jnp.float32)
    harmonic_y = (lattice_y - modes_y // 2).astype(jnp.float32)
    cosine_x, sine_x = phase_table(position_x, harmonic_x)
    cosine_y, sine_y = phase_table(position_y, harmonic_y)
    weight_rows = jnp.take(spectral_weight, frequency, axis=0)
    factor = weight_rows * (1.0 / math.sqrt(modes_x * modes_y * panels))
    factor_wide = jnp.transpose(factor, (1, 0, 2)).reshape(modes_x, vectors * modes_y)[:, None, :]

    def near_field(density):
        padded = padded_2(density, (("tile", 0), ("wave", 1)), 1)
        candidates = []
        for slot_index in range(9):
            shift_x = slot_index // 3 - 1
            shift_y = slot_index % 3 - 1
            candidates.append(
                padded[1 + shift_x : 1 + shift_x + strips, 1 + shift_y : 1 + shift_y + tiles_y]
            )
        stacked = jnp.stack(candidates, 2).reshape(strips * tiles_y, 9, -1)
        picked = jnp.take_along_axis(stacked, neighbor.reshape(strips * tiles_y, 9, 1), axis=1)
        picked = picked.reshape(strips * tiles_y, 9, 2 * vectors, panels_t)
        blocks = kernel.reshape(strips * tiles_y, 9, 2, panels_t, panels_t)
        product = jnp.einsum("tjmp,tjcpq->tcmq", picked, blocks, preferred_element_type=jnp.float32)
        return combine_near(product, vectors).reshape(strips, tiles_y, 2, vectors, panels_t)

    def far_field(density):
        panel_density = jnp.transpose(density, (0, 1, 4, 2, 3)).reshape(local_rows, 2, vectors)
        twisted = twist_density(panel_density, cosine_y, sine_y)
        partial_coeffs = project_rows(cosine_x, sine_x, twisted)
        share_rows = modes_x // devices
        shares = lax.psum_scatter(partial_coeffs, ("tile", "wave"), scatter_dimension=0, tiled=True)
        owner_index = lax.axis_index("tile") * lax.axis_size("wave") + lax.axis_index("wave")
        owner_factor = lax.dynamic_slice_in_dim(
            factor_wide, owner_index * share_rows, share_rows, 0
        )
        owner_scaled = (shares * owner_factor).astype(jnp.bfloat16)
        scaled = lax.all_gather(owner_scaled, ("tile", "wave"), axis=0, tiled=True)
        summed = expand_rows(cosine_x, sine_x, scaled)
        far_panel = finish(summed, cosine_y, sine_y, vectors)
        return far_panel.reshape(strips, tiles_y, panels_t, 2, vectors).transpose(0, 1, 3, 4, 2)

    def apply_operator(density):
        return 0.5 * density.astype(jnp.float32) + near_field(density) + far_field(density)

    local_sq = panel_sum(
        residual[:, :, 0] * residual[:, :, 0] + residual[:, :, 1] * residual[:, :, 1]
    )
    squares = lax.psum(local_sq, ("tile", "wave"))
    basis_scale = jnp.sqrt(squares / panels + eps_norm)
    basis_one = (residual / basis_scale[None, None, None, :, None]).astype(jnp.bfloat16)
    image_one = apply_operator(basis_one)
    basis_real = basis_one[:, :, 0].astype(jnp.float32)
    basis_imag = basis_one[:, :, 1].astype(jnp.float32)
    image_real = image_one[:, :, 0]
    image_imag = image_one[:, :, 1]
    inner_real, inner_imag = lax.psum(
        (
            panel_sum(basis_real * image_real + basis_imag * image_imag),
            panel_sum(basis_real * image_imag - basis_imag * image_real),
        ),
        ("tile", "wave"),
    )
    coef_real = inner_real / panels
    coef_imag = inner_imag / panels
    wide_real = coef_real[None, None, :, None]
    wide_imag = coef_imag[None, None, :, None]
    update_real = image_real - (wide_real * basis_real - wide_imag * basis_imag)
    update_imag = image_imag - (wide_real * basis_imag + wide_imag * basis_real)
    update_sq = lax.psum(
        panel_sum(update_real * update_real + update_imag * update_imag), ("tile", "wave")
    )
    update_scale = jnp.sqrt(update_sq / panels + eps_norm)
    next_basis = (
        jnp.stack([update_real, update_imag], 2) / update_scale[None, None, None, :, None]
    ).astype(jnp.bfloat16)
    image_two = apply_operator(next_basis)
    arnoldi = jnp.stack([basis_scale, coef_real, coef_imag, update_scale])
    return (image_two, arnoldi)


def solution(mesh):
    return jax.shard_map(
        per_device,
        mesh=mesh,
        in_specs=(
            P(("grp", "tile"), "wave", None, None, None),
            P(("grp", "tile"), "wave", None, None, None, None),
            P(("grp", "tile"), "wave", None, None),
            P(("grp", "tile"), "wave", None),
            P("grp"),
            P(),
            P(),
            P(),
        ),
        out_specs=(P(("grp", "tile"), "wave", None, None, None), P("grp", None)),
        check_vma=False,
    )
```

profile of v0, /device:TPU:0, one launch (start us, length us, event | category | flops | bytes accessed | tf_op | source)
XLA Modules:
  0.0 307.0 jit_solution(9363511399105179548)
XLA Ops:
  7.2 1.0 add_reduce_fusion.2
  8.2 34.9 %psum.28 = f32[8]{0:T(128)S(1)} all-reduce(f32[8]{0:T(128)S(1)} %add_reduce_fusion.2), channel_id=1, replica_groups=mesh['grp'=2,'tile'=8,'wave'=2] {'tile','wave'}, use_global_device_ids=true, to_apply=%region_1.2 | all-reduce | flops 8 | bytes 64 | tf_op jit(solution)/shard_map/psum | solution.py:149
  43.7 1.4 fusion.22
  45.2 4.7 %collective-permute-start.1 = (bf16[1,4,2,8,128]{4,3,1,2,0:T(8,128)(2,1)}, bf16[1,4,2,8,128]{4,3,1,2,0:T(8,128)(2,1)}, u32[]{:S(2)}, u32[]{:S(2)}) collective-permute-start(bf16[1,4,2,8,128]{4,3,1,2,0:T(8,128)(2,1)} %fusion.22), channel_id=1, source_target_pairs={{2,0},{4,2},{6,4},{8,6},{10,8},{12,10},{14,12},{0,14},{3,1},{5,3},... | collective-permute-start | bytes 49160 | tf_op jit(solution)/shard_map/ppermute | solution.py:19
  49.9 0.8 fusion.72
  52.1 0.8 fusion.63
  52.9 1.0 fusion.16
  54.7 1.1 cosine_convert_fusion.1
  56.9 1.1 pad_maximum_fusion.2
  58.7 1.6 gather_fusion
  60.3 0.9 multiply_bitcast_fusion
  61.7 1.2 copy.121
  63.0 1.3 pad_maximum_fusion.31
  64.3 1.0 constant_dynamic-slice_fusion
  65.3 0.8 copy.126
  66.2 0.9 copy.128
  67.8 1.2 copy.122
  69.0 0.8 reshape.723
  71.8 0.8 pad_maximum_fusion.21
  73.7 1.5 gather_fusion.1
  76.5 36.3 %reduce-scatter.3.cloned.1.call-done = f32[8,2,1024]{2,0,1:T(8,128)} async-done(((f32[128,2,1024]{2,0,1:T(8,128)}), f32[8,2,1024]{2,0,1:T(8,128)}) %reduce-scatter.3.cloned.1.call-update) | async-done | bytes 65552 | tf_op jit(solution)/shard_map/reduce_scatter | solution.py:132
  112.8 0.8 multiply_convert_fusion.1
  113.7 20.8 %all_gather.6 = bf16[128,2,1024]{2,0,1:T(8,128)(2,1)S(1)} all-gather(bf16[8,2,1024]{2,0,1:T(8,128)(2,1)S(1)} %multiply_convert_fusion.1), channel_id=1, replica_groups=mesh['grp'=2,'tile'=8,'wave'=2] {'tile','wave'}, dimensions={0}, use_global_device_ids=true | all-gather | bytes 557056 | tf_op jit(solution)/shard_map/all_gather | solution.py:138
  134.4 0.8 slice_negate_fusion.1
  135.3 1.0 copy.123
  136.3 1.1 pad_maximum_fusion.4
  137.4 1.0 copy.124
  138.4 2.0 convolution_bitcast_fusion.1
  140.4 0.9 copy.178
  141.4 1.2 subtract_reduce_fusion.1
  143.4 0.9 fusion.19
  144.3 0.9 fusion.33
  145.2 29.8 %all-reduce = (f32[8]{0:T(128)S(1)}, f32[8]{0:T(128)S(1)}) all-reduce(f32[8]{0:T(128)S(1)} %get-tuple-element.16, f32[8]{0:T(128)S(1)} %get-tuple-element.15), channel_id=1, replica_groups=mesh['grp'=2,'tile'=8,'wave'=2] {'tile','wave'}, use_global_device_ids=true, to_apply=%region_8.10 | all-reduce | flops 16 | bytes 128 | tf_op jit(solution)/shard_map/psum | solution.py:157
  175.0 0.9 fusion.40
  175.9 0.8 fusion.45
  176.7 29.5 %psum.31 = f32[8]{0:T(128)S(1)} all-reduce(f32[8]{0:T(128)S(1)} %fusion.40), channel_id=1, replica_groups=mesh['grp'=2,'tile'=8,'wave'=2] {'tile','wave'}, use_global_device_ids=true, to_apply=%region_10.12 | all-reduce | flops 8 | bytes 64 | tf_op jit(solution)/shard_map/psum | solution.py:170
  206.4 4.7 %collective-permute-start.5 = (bf16[1,4,2,8,128]{4,3,1,2,0:T(8,128)(2,1)S(1)}, bf16[1,4,2,8,128]{4,3,1,2,0:T(8,128)(2,1)S(1)}, u32[]{:S(2)}, u32[]{:S(2)}) collective-permute-start(bf16[1,4,2,8,128]{4,3,1,2,0:T(8,128)(2,1)S(1)} %fusion.20), channel_id=1, source_target_pairs={{2,0},{4,2},{6,4},{8,6},{10,8},{12,10},{14,12},{0,14},{3,1},{5,3},... | collective-permute-start | bytes 49160 | tf_op jit(solution)/shard_map/ppermute | solution.py:19
  213.7 1.1 pad_maximum_fusion.3
  217.2 1.5 gather_fusion.2
  219.4 50.2 %reduce-scatter.5.cloned.1.call-done = f32[8,2,1024]{2,0,1:T(8,128)} async-done(((f32[128,2,1024]{2,0,1:T(8,128)}), f32[8,2,1024]{2,0,1:T(8,128)}) %reduce-scatter.5.cloned.1.call-update) | async-done | bytes 65552 | tf_op jit(solution)/shard_map/reduce_scatter | solution.py:132
  269.6 0.8 multiply_convert_fusion
  270.5 20.8 %all_gather.7 = bf16[128,2,1024]{2,0,1:T(8,128)(2,1)S(1)} all-gather(bf16[8,2,1024]{2,0,1:T(8,128)(2,1)S(1)} %multiply_convert_fusion), channel_id=1, replica_groups=mesh['grp'=2,'tile'=8,'wave'=2] {'tile','wave'}, dimensions={0}, use_global_device_ids=true | all-gather | bytes 557056 | tf_op jit(solution)/shard_map/all_gather | solution.py:138
  292.0 1.0 copy.147
  293.0 1.0 pad_maximum_fusion.5
  294.0 1.0 copy.148
  295.1 2.0 convolution_bitcast_fusion
  297.0 0.9 copy.179
  298.1 1.2 subtract_reduce_fusion
  (173 shorter events, 18.3 us)
Async XLA Ops:
  7.2 68.3 %copy-start = (bf16[1,4,9,2,128,128]{5,4,3,2,1,0:T(8,128)(2,1)S(1)}, bf16[1,4,9,2,128,128]{5,4,3,2,1,0:T(8,128)(2,1)}, u32[]{:S(2)}) copy-start(bf16[1,4,9,2,128,128]{5,4,3,2,1,0:T(8,128)(2,1)} %param.11) | copy-start | bytes 7077892
  7.2 105.6 %reduce-scatter.3.cloned.1.call-start = ((), (), s32[]{:S(2)}) async-start(), calls=%async_computation.2 | async-start | bytes 1114112 | tf_op jit(solution)/shard_map/reduce_scatter | solution.py:132
  43.7 7.0 %copy-start.19 = (f32[8]{0:T(128)}, f32[8]{0:T(128)S(1)}, u32[]{:S(2)}) copy-start(f32[8]{0:T(128)S(1)} %get-tuple-element.68) | copy-start | bytes 100
  45.2 17.8 %collective-permute-start = (bf16[1,4,2,8,128]{4,3,1,2,0:T(8,128)(2,1)}, bf16[1,4,2,8,128]{4,3,1,2,0:T(8,128)(2,1)}, u32[]{:S(2)}, u32[]{:S(2)}) collective-permute-start(bf16[1,4,2,8,128]{4,3,1,2,0:T(8,128)(2,1)} %fusion.22), channel_id=1, source_target_pairs={{0,2},{2,4},{4,6},{6,8},{8,10},{10,12},{12,14},{14,0},{1,3},{3,5},... | collective-permute-start | bytes 49160 | tf_op jit(solution)/shard_map/ppermute | solution.py:18
  45.2 17.8 %collective-permute-start.1 = (bf16[1,4,2,8,128]{4,3,1,2,0:T(8,128)(2,1)}, bf16[1,4,2,8,128]{4,3,1,2,0:T(8,128)(2,1)}, u32[]{:S(2)}, u32[]{:S(2)}) collective-permute-start(bf16[1,4,2,8,128]{4,3,1,2,0:T(8,128)(2,1)} %fusion.22), channel_id=1, source_target_pairs={{2,0},{4,2},{6,4},{8,6},{10,8},{12,10},{14,12},{0,14},{3,1},{5,3},... | collective-permute-start | bytes 49160 | tf_op jit(solution)/shard_map/ppermute | solution.py:19
  53.9 12.3 %copy-start.1 = (f32[512,128]{0,1:T(8,128)}, f32[512,128]{0,1:T(8,128)S(1)}, u32[]{:S(2)}) copy-start(f32[512,128]{0,1:T(8,128)S(1)} %get-tuple-element.64) | copy-start | bytes 786436
  55.8 0.8 copy-start.9
  55.9 0.8 copy-start.7
  56.9 1.2 copy-start.24
  56.9 1.2 copy-start.18
  58.0 211.7 %reduce-scatter.5.cloned.1.call-start = ((), (), s32[]{:S(2)}) async-start(), calls=%async_computation.3 | async-start | bytes 1114112 | tf_op jit(solution)/shard_map/reduce_scatter | solution.py:132
  64.3 7.5 %collective-permute-start.2 = (bf16[3,1,2,8,128]{4,3,1,2,0:T(8,128)(2,1)}, bf16[3,1,2,8,128]{4,3,1,2,0:T(8,128)(2,1)}, u32[]{:S(2)}, u32[]{:S(2)}) collective-permute-start(bf16[3,1,2,8,128]{4,3,1,2,0:T(8,128)(2,1)} %get-tuple-element.56), channel_id=1, source_target_pairs={{0,1},{1,0},{2,3},{3,2},{4,5},{5,4},{6,7},{7,6},{8,9},{9,8},{10,11... | collective-permute-start | bytes 36872 | tf_op jit(solution)/shard_map/ppermute | solution.py:18
  67.7 7.5 %copy-start.21 = (pred[4,9]{1,0:T(4,128)(4,1)S(1)}, pred[4,9]{1,0:T(4,128)(4,1)}, u32[]{:S(2)}) copy-start(pred[4,9]{1,0:T(4,128)(4,1)} %and_bitcast_fusion) | copy-start | bytes 112
  69.0 43.9 %copy-start.16 = (f32[8,1,1024]{2,0,1:T(8,128)}, f32[8,1,1024]{2,0,1:T(8,128)S(1)}, u32[]{:S(2)}) copy-start(f32[8,1,1024]{2,0,1:T(8,128)S(1)} %copy.122) | copy-start | bytes 98308
  70.5 2.1 collective-permute-start.3
  134.4 4.0 %copy-start.10 = (bf16[512,128]{0,1:T(8,128)(2,1)S(1)}, bf16[512,128]{0,1:T(8,128)(2,1)}, u32[]{:S(2)}) copy-start(bf16[512,128]{0,1:T(8,128)(2,1)} %copy-done.9) | copy-start | bytes 393220
  140.4 1.0 copy-start.3
  140.4 1.0 copy-start.5
  141.4 2.0 copy-start.20
  141.4 69.8 %copy-start.2 = (f32[512,128]{0,1:T(8,128)S(1)}, f32[512,128]{0,1:T(8,128)}, u32[]{:S(2)}) copy-start(f32[512,128]{0,1:T(8,128)} %copy-done.1) | copy-start | bytes 786436
  176.7 38.0 %copy-start.12 = (f32[1,4,1,8,128]{4,3,1,2,0:T(8,128)}, f32[1,4,1,8,128]{4,3,1,2,0:T(8,128)S(1)}, u32[]{:S(2)}) copy-start(f32[1,4,1,8,128]{4,3,1,2,0:T(8,128)S(1)} %get-tuple-element.51) | copy-start | bytes 49156
  176.7 38.0 %copy-start.14 = (f32[1,4,1,8,128]{4,3,1,2,0:T(8,128)}, f32[1,4,1,8,128]{4,3,1,2,0:T(8,128)S(1)}, u32[]{:S(2)}) copy-start(f32[1,4,1,8,128]{4,3,1,2,0:T(8,128)S(1)} %get-tuple-element.52) | copy-start | bytes 49156
  206.4 8.4 %collective-permute-start.4 = (bf16[1,4,2,8,128]{4,3,1,2,0:T(8,128)(2,1)S(1)}, bf16[1,4,2,8,128]{4,3,1,2,0:T(8,128)(2,1)S(1)}, u32[]{:S(2)}, u32[]{:S(2)}) collective-permute-start(bf16[1,4,2,8,128]{4,3,1,2,0:T(8,128)(2,1)S(1)} %fusion.20), channel_id=1, source_target_pairs={{0,2},{2,4},{4,6},{6,8},{8,10},{10,12},{12,14},{14,0},{1,3},{3,5},... | collective-permute-start | bytes 49160 | tf_op jit(solution)/shard_map/ppermute | solution.py:18
  206.4 8.4 %collective-permute-start.5 = (bf16[1,4,2,8,128]{4,3,1,2,0:T(8,128)(2,1)S(1)}, bf16[1,4,2,8,128]{4,3,1,2,0:T(8,128)(2,1)S(1)}, u32[]{:S(2)}, u32[]{:S(2)}) collective-permute-start(bf16[1,4,2,8,128]{4,3,1,2,0:T(8,128)(2,1)S(1)} %fusion.20), channel_id=1, source_target_pairs={{2,0},{4,2},{6,4},{8,6},{10,8},{12,10},{14,12},{0,14},{3,1},{5,3},... | collective-permute-start | bytes 49160 | tf_op jit(solution)/shard_map/ppermute | solution.py:19
  211.8 1.0 copy-start.8
  213.7 1.3 copy-start.23
  214.8 4.0 %copy-start.22 = (pred[4,9]{1,0:T(4,128)(4,1)S(1)}, pred[4,9]{1,0:T(4,128)(4,1)}, u32[]{:S(2)}) copy-start(pred[4,9]{1,0:T(4,128)(4,1)} %and_bitcast_fusion) | copy-start | bytes 112
  214.8 1.2 collective-permute-start.7
  215.5 1.3 collective-permute-start.6
  218.7 51.0 %copy-start.17 = (f32[8,1,1024]{2,0,1:T(8,128)S(1)}, f32[8,1,1024]{2,0,1:T(8,128)}, u32[]{:S(2)}) copy-start(f32[8,1,1024]{2,0,1:T(8,128)} %copy-done.16) | copy-start | bytes 98308
  291.3 3.8 %copy-start.11 = (bf16[512,128]{0,1:T(8,128)(2,1)S(1)}, bf16[512,128]{0,1:T(8,128)(2,1)}, u32[]{:S(2)}) copy-start(bf16[512,128]{0,1:T(8,128)(2,1)} %copy-done.9) | copy-start | bytes 393220
  297.0 1.0 copy-start.4
  297.0 1.0 copy-start.6
  298.0 1.4 copy-start.13
  298.0 1.4 copy-start.15
Sparse Core Ops, SparseCore 0:
  58.1 54.6 reduce-scatter.2
  214.9 54.7 reduce-scatter.4
where the time goes:
time: 308 us; the launch traced here: 307 us
  blocking collectives  136 us (44%)
  waiting for transfers between devices  87.3 us (28%)
  other arithmetic  30 us (10%)
  local copies, waits for them, and re-layouts  22.2 us (7%)
  between operations  14.9 us (5%)
  starting transfers between devices  10.7 us (3%)
  matrix products  6.26 us (2%)
    reduce_scatter x2, waiting for transfers between devices, far_field(): lax.psum_scatter(partial_coeffs, ('tile', 'wave'), scatter_dimension=0, t...  86.5 us
    all_gather x2, blocking collectives, far_field(): scaled = lax.all_gather(owner_scaled, ('tile', 'wave'), axis=0, tiled=True)  41.5 us
    psum x1, blocking collectives, per_device(): squares = lax.psum(local_sq, ('tile', 'wave'))  34.9 us
    psum x1, blocking collectives, per_device(): lax.psum((panel_sum(basis_real * image_real + basis_imag * image_imag), p...  29.8 us
    psum x1, blocking collectives, per_device(): lax.psum(panel_sum(update_real * update_real + update_imag * update_imag)...  29.5 us
    ppermute x4, starting transfers between devices, padded_2(): after = lax.ppermute(initial, axis, down)  10.1 us
  transfers between devices with their start and end apart: 10, of which 3 were waited for; matrix products, arithmetic and copies ran while one was open for 10% of the time, Pallas kernels for 0%

commit v1 on v0

--- a/solution.py
+++ b/solution.py
@@ -135,7 +135,31 @@
             factor_wide, owner_index * share_rows, share_rows, 0
         )
         owner_scaled = (shares * owner_factor).astype(jnp.bfloat16)
-        scaled = lax.all_gather(owner_scaled, ("tile", "wave"), axis=0, tiled=True)
+        ways, here, step = (
+            lax.axis_size(("tile", "wave")),
+            lax.axis_index(("tile", "wave")),
+            owner_scaled.shape[0],
+        )
+        dims = [n * ways if d == 0 else n for d, n in enumerate(owner_scaled.shape)]
+        full = lax.dynamic_update_slice_in_dim(
+            jnp.zeros(dims, owner_scaled.dtype), owner_scaled, here * step, axis=0
+        )
+        going_up = going_down = owner_scaled
+        for far in range(1, ways // 2 + 1):
+            going_up = lax.ppermute(
+                going_up, ("tile", "wave"), [(d, (d + 1) % ways) for d in range(ways)]
+            )
+            full = lax.dynamic_update_slice_in_dim(
+                full, going_up, (here - far) % ways * step, axis=0
+            )
+            if 2 * far < ways:
+                going_down = lax.ppermute(
+                    going_down, ("tile", "wave"), [(d, (d - 1) % ways) for d in range(ways)]
+                )
+                full = lax.dynamic_update_slice_in_dim(
+                    full, going_down, (here + far) % ways * step, axis=0
+                )
+        scaled = full
         summed = expand_rows(cosine_x, sine_x, scaled)
         far_panel = finish(summed, cosine_y, sine_y, vectors)
         return far_panel.reshape(strips, tiles_y, panels_t, 2, vectors).transpose(0, 1, 3, 4, 2)

time: 308 us -> 582 us (1.89); the launches traced: 307 us -> 571 us
  local copies, waits for them, and re-layouts: 22.2 us -> 241 us
  starting transfers between devices: 10.7 us -> 73.3 us
  blocking collectives: 136 us -> 98.3 us
  waiting for transfers between devices: 87.3 us -> 108 us
    dynamic_update_slice x0 -> x32, local copies, waits for them, and re-layouts: none -> 185 us  [the longest x16 93.6 us: far_field(): lax.dynamic_update_slice_in_dim(full, going_up, (here - far) % ways * ste...]
    ppermute x0 -> x30, starting transfers between devices: none -> 62.6 us  [the longest x14 62.4 us: far_field(): lax.ppermute(going_down, ('tile', 'wave'), [(d, (d - 1) % ways) for d in...]
    all_gather x2 -> x0, blocking collectives: 41.5 us -> none  [far_field(): scaled = lax.all_gather(owner_scaled, ('tile', 'wave'), axis=0, tiled=True)]
    ppermute x0 -> x30, local copies, waits for them, and re-layouts: none -> 37.3 us  [the longest x16 21.6 us: far_field(): lax.ppermute(going_up, ('tile', 'wave'), [(d, (d + 1) % ways) for d in ra...]
    ppermute x0 -> x30, waiting for transfers between devices: none -> 18.4 us  [the longest x16 12 us: far_field(): lax.ppermute(going_up, ('tile', 'wave'), [(d, (d + 1) % ways) for d in ra...]
  transfers between devices with their start and end apart: 10 -> 40, of which waited for: 3 -> 24; matrix products, arithmetic and copies ran while one was open for 10% -> 43% of each run, Pallas kernels for 0% -> 0%
where the time goes in v1:
time: 582 us; the launch traced here: 571 us
  local copies, waits for them, and re-layouts  241 us (41%)
  waiting for transfers between devices  108 us (19%)
  blocking collectives  98.3 us (17%)
  starting transfers between devices  73.3 us (13%)
  other arithmetic  32.1 us (6%)
  between operations  15.4 us (3%)
    dynamic_update_slice x16, local copies, waits for them, and re-layouts, far_field(): lax.dynamic_update_slice_in_dim(full, going_up, (here - far) % ways * ste...  93.6 us
    reduce_scatter x2, waiting for transfers between devices, far_field(): lax.psum_scatter(partial_coeffs, ('tile', 'wave'), scatter_dimension=0, t...  88.3 us
    dynamic_update_slice x14, local copies, waits for them, and re-layouts, far_field(): lax.dynamic_update_slice_in_dim(full, going_down, (here + far) % ways * s...  81.6 us
    ppermute x14, starting transfers between devices, far_field(): lax.ppermute(going_down, ('tile', 'wave'), [(d, (d - 1) % ways) for d in...  62.4 us
    psum x1, blocking collectives, per_device(): squares = lax.psum(local_sq, ('tile', 'wave'))  34.9 us
    psum x1, blocking collectives, per_device(): lax.psum((panel_sum(basis_real * image_real + basis_imag * image_imag), p...  33.9 us
    psum x1, blocking collectives, per_device(): lax.psum(panel_sum(update_real * update_real + update_imag * update_imag)...  29.5 us
    ppermute x16, local copies, waits for them, and re-layouts, far_field(): lax.ppermute(going_up, ('tile', 'wave'), [(d, (d + 1) % ways) for d in ra...  21.6 us
  transfers between devices with their start and end apart: 40, of which 24 were waited for; matrix products, arithmetic and copies ran while one was open for 43% of the time, Pallas kernels for 0%

profile of v1, /device:TPU:0, one launch (start us, length us, event | category | flops | bytes accessed | tf_op | source)
XLA Modules:
  0.0 571.5 jit_solution(10209974635053442312)
XLA Ops:
  8.2 34.9 %psum.28 = f32[8]{0:T(128)S(1)} all-reduce(f32[8]{0:T(128)S(1)} %add_reduce_fusion.2), channel_id=1, replica_groups=mesh['grp'=2,'tile'=8,'wave'=2] {'tile','wave'}, use_global_device_ids=true, to_apply=%region_1.2 | all-reduce | flops 8 | bytes 64 | tf_op jit(solution)/shard_map/psum | solution.py:173
  44.6 4.7 collective-permute-start.1
  76.4 35.9 %reduce-scatter.3.cloned.1.call-done = f32[8,2,1024]{2,0,1:T(8,128)} async-done(((f32[128,2,1024]{2,0,1:T(8,128)}), f32[8,2,1024]{2,0,1:T(8,128)}) %reduce-scatter.3.cloned.1.call-update) | async-done | bytes 65552 | tf_op jit(solution)/shard_map/reduce_scatter | solution.py:132
  113.2 4.5 collective-permute-start.5
  119.3 4.4 collective-permute-start.7
  125.4 4.5 collective-permute-start.9
  133.1 4.5 collective-permute-start.11
  139.2 4.5 collective-permute-start.13
  151.6 4.4 collective-permute-start.17
  158.5 4.8 dynamic_update_slice.96
  164.3 5.8 %dynamic_update_slice.97 = bf16[128,2,1024]{0,2,1:T(8,128)(2,1)S(1)} dynamic-update-slice(bf16[128,2,1024]{0,2,1:T(8,128)(2,1)S(1)} %dynamic_update_slice.96, bf16[8,2,1024]{0,2,1:T(8,128)(2,1)} %copy.180, s32[]{:T(128)S(6)} %select_n.180, s32[]{:T(128)} %constant.169.clone.1, s32[]{:T(128)} %constant.169.clone.1) | dynamic-update-slice | bytes 65540 | tf_op jit(solution)/shard_map/dynamic_update_slice | solution.py:152
  171.2 5.8 %dynamic_update_slice.98 = bf16[128,2,1024]{0,2,1:T(8,128)(2,1)S(1)} dynamic-update-slice(bf16[128,2,1024]{0,2,1:T(8,128)(2,1)S(1)} %dynamic_update_slice.97, bf16[8,2,1024]{0,2,1:T(8,128)(2,1)} %copy.181, s32[]{:T(128)S(6)} %select_n.182, s32[]{:T(128)} %constant.169.clone.1, s32[]{:T(128)} %constant.169.clone.1) | dynamic-update-slice | bytes 65540 | tf_op jit(solution)/shard_map/dynamic_update_slice | solution.py:159
  178.0 5.8 %dynamic_update_slice.99 = bf16[128,2,1024]{0,2,1:T(8,128)(2,1)S(1)} dynamic-update-slice(bf16[128,2,1024]{0,2,1:T(8,128)(2,1)S(1)} %dynamic_update_slice.98, bf16[8,2,1024]{0,2,1:T(8,128)(2,1)} %copy.182, s32[]{:T(128)S(6)} %select_n.184, s32[]{:T(128)} %constant.169.clone.1, s32[]{:T(128)} %constant.169.clone.1) | dynamic-update-slice | bytes 65540 | tf_op jit(solution)/shard_map/dynamic_update_slice | solution.py:152
  184.9 5.8 %dynamic_update_slice.100 = bf16[128,2,1024]{0,2,1:T(8,128)(2,1)S(1)} dynamic-update-slice(bf16[128,2,1024]{0,2,1:T(8,128)(2,1)S(1)} %dynamic_update_slice.99, bf16[8,2,1024]{0,2,1:T(8,128)(2,1)} %copy.183, s32[]{:T(128)S(6)} %select_n.186, s32[]{:T(128)} %constant.169.clone.1, s32[]{:T(128)} %constant.169.clone.1) | dynamic-update-slice | bytes 65540 | tf_op jit(solution)/shard_map/dynamic_update_slice | solution.py:159
  192.5 5.8 %dynamic_update_slice.101 = bf16[128,2,1024]{0,2,1:T(8,128)(2,1)S(1)} dynamic-update-slice(bf16[128,2,1024]{0,2,1:T(8,128)(2,1)S(1)} %dynamic_update_slice.100, bf16[8,2,1024]{0,2,1:T(8,128)(2,1)} %copy.184, s32[]{:T(128)S(6)} %select_n.188, s32[]{:T(128)} %constant.169.clone.1, s32[]{:T(128)} %constant.169.clone.1) | dynamic-update-slice | bytes 65540 | tf_op jit(solution)/shard_map/dynamic_update_slice | solution.py:152
  199.3 5.8 %dynamic_update_slice.102 = bf16[128,2,1024]{0,2,1:T(8,128)(2,1)S(1)} dynamic-update-slice(bf16[128,2,1024]{0,2,1:T(8,128)(2,1)S(1)} %dynamic_update_slice.101, bf16[8,2,1024]{0,2,1:T(8,128)(2,1)} %copy.185, s32[]{:T(128)S(6)} %select_n.190, s32[]{:T(128)} %constant.169.clone.1, s32[]{:T(128)} %constant.169.clone.1) | dynamic-update-slice | bytes 65540 | tf_op jit(solution)/shard_map/dynamic_update_slice | solution.py:159
  207.0 5.8 %dynamic_update_slice.103 = bf16[128,2,1024]{0,2,1:T(8,128)(2,1)S(1)} dynamic-update-slice(bf16[128,2,1024]{0,2,1:T(8,128)(2,1)S(1)} %dynamic_update_slice.102, bf16[8,2,1024]{0,2,1:T(8,128)(2,1)} %copy.186, s32[]{:T(128)S(6)} %select_n.192, s32[]{:T(128)} %constant.169.clone.1, s32[]{:T(128)} %constant.169.clone.1) | dynamic-update-slice | bytes 65540 | tf_op jit(solution)/shard_map/dynamic_update_slice | solution.py:152
  214.6 5.8 %dynamic_update_slice.104 = bf16[128,2,1024]{0,2,1:T(8,128)(2,1)S(1)} dynamic-update-slice(bf16[128,2,1024]{0,2,1:T(8,128)(2,1)S(1)} %dynamic_update_slice.103, bf16[8,2,1024]{0,2,1:T(8,128)(2,1)} %copy.187, s32[]{:T(128)S(6)} %select_n.194, s32[]{:T(128)} %constant.169.clone.1, s32[]{:T(128)} %constant.169.clone.1) | dynamic-update-slice | bytes 65540 | tf_op jit(solution)/shard_map/dynamic_update_slice | solution.py:159
  222.2 5.8 %dynamic_update_slice.105 = bf16[128,2,1024]{0,2,1:T(8,128)(2,1)S(1)} dynamic-update-slice(bf16[128,2,1024]{0,2,1:T(8,128)(2,1)S(1)} %dynamic_update_slice.104, bf16[8,2,1024]{0,2,1:T(8,128)(2,1)} %copy.188, s32[]{:T(128)S(6)} %select_n.196, s32[]{:T(128)} %constant.169.clone.1, s32[]{:T(128)} %constant.169.clone.1) | dynamic-update-slice | bytes 65540 | tf_op jit(solution)/shard_map/dynamic_update_slice | solution.py:152
  229.0 5.8 %dynamic_update_slice.106 = bf16[128,2,1024]{0,2,1:T(8,128)(2,1)S(1)} dynamic-update-slice(bf16[128,2,1024]{0,2,1:T(8,128)(2,1)S(1)} %dynamic_update_slice.105, bf16[8,2,1024]{0,2,1:T(8,128)(2,1)} %copy.189, s32[]{:T(128)S(6)} %select_n.198, s32[]{:T(128)} %constant.169.clone.1, s32[]{:T(128)} %constant.169.clone.1) | dynamic-update-slice | bytes 65540 | tf_op jit(solution)/shard_map/dynamic_update_slice | solution.py:159
  235.9 5.8 %dynamic_update_slice.107 = bf16[128,2,1024]{0,2,1:T(8,128)(2,1)S(1)} dynamic-update-slice(bf16[128,2,1024]{0,2,1:T(8,128)(2,1)S(1)} %dynamic_update_slice.106, bf16[8,2,1024]{0,2,1:T(8,128)(2,1)} %copy.190, s32[]{:T(128)S(6)} %select_n.200, s32[]{:T(128)} %constant.169.clone.1, s32[]{:T(128)} %constant.169.clone.1) | dynamic-update-slice | bytes 65540 | tf_op jit(solution)/shard_map/dynamic_update_slice | solution.py:152
  242.7 5.8 %dynamic_update_slice.108 = bf16[128,2,1024]{0,2,1:T(8,128)(2,1)S(1)} dynamic-update-slice(bf16[128,2,1024]{0,2,1:T(8,128)(2,1)S(1)} %dynamic_update_slice.107, bf16[8,2,1024]{0,2,1:T(8,128)(2,1)} %copy.191, s32[]{:T(128)S(6)} %select_n.202, s32[]{:T(128)} %constant.169.clone.1, s32[]{:T(128)} %constant.169.clone.1) | dynamic-update-slice | bytes 65540 | tf_op jit(solution)/shard_map/dynamic_update_slice | solution.py:159
  250.3 6.0 %dynamic_update_slice.109 = bf16[128,2,1024]{0,2,1:T(8,128)(2,1)S(1)} dynamic-update-slice(bf16[128,2,1024]{0,2,1:T(8,128)(2,1)S(1)} %dynamic_update_slice.108, bf16[8,2,1024]{0,2,1:T(8,128)(2,1)} %copy.192, s32[]{:T(128)S(6)} %select_n.204, s32[]{:T(128)} %constant.169.clone.1, s32[]{:T(128)} %constant.169.clone.1) | dynamic-update-slice | bytes 65540 | tf_op jit(solution)/shard_map/dynamic_update_slice | solution.py:152
  258.2 5.8 %dynamic_update_slice.110 = bf16[128,2,1024]{0,2,1:T(8,128)(2,1)S(1)} dynamic-update-slice(bf16[128,2,1024]{0,2,1:T(8,128)(2,1)S(1)} %dynamic_update_slice.109, bf16[8,2,1024]{0,2,1:T(8,128)(2,1)} %copy.193, s32[]{:T(128)S(6)} %select_n.206, s32[]{:T(128)} %constant.169.clone.1, s32[]{:T(128)} %constant.169.clone.1) | dynamic-update-slice | bytes 65540 | tf_op jit(solution)/shard_map/dynamic_update_slice | solution.py:159
  265.8 5.8 %dynamic_update_slice.111 = bf16[128,2,1024]{0,2,1:T(8,128)(2,1)S(1)} dynamic-update-slice(bf16[128,2,1024]{0,2,1:T(8,128)(2,1)S(1)} %dynamic_update_slice.110, bf16[8,2,1024]{0,2,1:T(8,128)(2,1)} %copy.194, s32[]{:T(128)S(6)} %select_n.208, s32[]{:T(128)} %constant.169.clone.1, s32[]{:T(128)} %constant.169.clone.1) | dynamic-update-slice | bytes 65540 | tf_op jit(solution)/shard_map/dynamic_update_slice | solution.py:152
  277.4 33.9 %all-reduce = (f32[8]{0:T(128)S(1)}, f32[8]{0:T(128)S(1)}) all-reduce(f32[8]{0:T(128)S(1)} %get-tuple-element.16, f32[8]{0:T(128)S(1)} %get-tuple-element.15), channel_id=1, replica_groups=mesh['grp'=2,'tile'=8,'wave'=2] {'tile','wave'}, use_global_device_ids=true, to_apply=%region_8.10 | all-reduce | flops 16 | bytes 128 | tf_op jit(solution)/shard_map/psum | solution.py:181
  313.0 29.5 %psum.31 = f32[8]{0:T(128)S(1)} all-reduce(f32[8]{0:T(128)S(1)} %fusion.40), channel_id=1, replica_groups=mesh['grp'=2,'tile'=8,'wave'=2] {'tile','wave'}, use_global_device_ids=true, to_apply=%region_10.12 | all-reduce | flops 8 | bytes 64 | tf_op jit(solution)/shard_map/psum | solution.py:194
  342.7 4.7 collective-permute-start.20
  353.4 52.4 %reduce-scatter.5.cloned.1.call-done = f32[8,2,1024]{2,0,1:T(8,128)} async-done(((f32[128,2,1024]{2,0,1:T(8,128)}), f32[8,2,1024]{2,0,1:T(8,128)}) %reduce-scatter.5.cloned.1.call-update) | async-done | bytes 65552 | tf_op jit(solution)/shard_map/reduce_scatter | solution.py:132
  406.7 4.5 collective-permute-start.24
  418.9 4.5 collective-permute-start.28
  426.4 4.5 collective-permute-start.30
  450.5 5.2 dynamic_update_slice.112
  456.7 5.8 %dynamic_update_slice.113 = bf16[128,2,1024]{0,2,1:T(8,128)(2,1)S(1)} dynamic-update-slice(bf16[128,2,1024]{0,2,1:T(8,128)(2,1)S(1)} %dynamic_update_slice.112, bf16[8,2,1024]{0,2,1:T(8,128)(2,1)} %copy.218, s32[]{:T(128)S(6)} %select_n.180, s32[]{:T(128)} %constant.169.clone.1, s32[]{:T(128)} %constant.169.clone.1) | dynamic-update-slice | bytes 65540 | tf_op jit(solution)/shard_map/dynamic_update_slice | solution.py:152
  463.6 5.8 %dynamic_update_slice.114 = bf16[128,2,1024]{0,2,1:T(8,128)(2,1)S(1)} dynamic-update-slice(bf16[128,2,1024]{0,2,1:T(8,128)(2,1)S(1)} %dynamic_update_slice.113, bf16[8,2,1024]{0,2,1:T(8,128)(2,1)} %copy.219, s32[]{:T(128)S(6)} %select_n.182, s32[]{:T(128)} %constant.169.clone.1, s32[]{:T(128)} %constant.169.clone.1) | dynamic-update-slice | bytes 65540 | tf_op jit(solution)/shard_map/dynamic_update_slice | solution.py:159
  470.4 5.8 %dynamic_update_slice.115 = bf16[128,2,1024]{0,2,1:T(8,128)(2,1)S(1)} dynamic-update-slice(bf16[128,2,1024]{0,2,1:T(8,128)(2,1)S(1)} %dynamic_update_slice.114, bf16[8,2,1024]{0,2,1:T(8,128)(2,1)} %copy.220, s32[]{:T(128)S(6)} %select_n.184, s32[]{:T(128)} %constant.169.clone.1, s32[]{:T(128)} %constant.169.clone.1) | dynamic-update-slice | bytes 65540 | tf_op jit(solution)/shard_map/dynamic_update_slice | solution.py:152
  477.3 5.8 %dynamic_update_slice.116 = bf16[128,2,1024]{0,2,1:T(8,128)(2,1)S(1)} dynamic-update-slice(bf16[128,2,1024]{0,2,1:T(8,128)(2,1)S(1)} %dynamic_update_slice.115, bf16[8,2,1024]{0,2,1:T(8,128)(2,1)} %copy.221, s32[]{:T(128)S(6)} %select_n.186, s32[]{:T(128)} %constant.169.clone.1, s32[]{:T(128)} %constant.169.clone.1) | dynamic-update-slice | bytes 65540 | tf_op jit(solution)/shard_map/dynamic_update_slice | solution.py:159
  484.1 5.8 %dynamic_update_slice.117 = bf16[128,2,1024]{0,2,1:T(8,128)(2,1)S(1)} dynamic-update-slice(bf16[128,2,1024]{0,2,1:T(8,128)(2,1)S(1)} %dynamic_update_slice.116, bf16[8,2,1024]{0,2,1:T(8,128)(2,1)} %copy.222, s32[]{:T(128)S(6)} %select_n.188, s32[]{:T(128)} %constant.169.clone.1, s32[]{:T(128)} %constant.169.clone.1) | dynamic-update-slice | bytes 65540 | tf_op jit(solution)/shard_map/dynamic_update_slice | solution.py:152
  491.0 5.8 %dynamic_update_slice.118 = bf16[128,2,1024]{0,2,1:T(8,128)(2,1)S(1)} dynamic-update-slice(bf16[128,2,1024]{0,2,1:T(8,128)(2,1)S(1)} %dynamic_update_slice.117, bf16[8,2,1024]{0,2,1:T(8,128)(2,1)} %copy.223, s32[]{:T(128)S(6)} %select_n.190, s32[]{:T(128)} %constant.169.clone.1, s32[]{:T(128)} %constant.169.clone.1) | dynamic-update-slice | bytes 65540 | tf_op jit(solution)/shard_map/dynamic_update_slice | solution.py:159
  497.8 5.8 %dynamic_update_slice.119 = bf16[128,2,1024]{0,2,1:T(8,128)(2,1)S(1)} dynamic-update-slice(bf16[128,2,1024]{0,2,1:T(8,128)(2,1)S(1)} %dynamic_update_slice.118, bf16[8,2,1024]{0,2,1:T(8,128)(2,1)} %copy.224, s32[]{:T(128)S(6)} %select_n.192, s32[]{:T(128)} %constant.169.clone.1, s32[]{:T(128)} %constant.169.clone.1) | dynamic-update-slice | bytes 65540 | tf_op jit(solution)/shard_map/dynamic_update_slice | solution.py:152
  504.7 5.8 %dynamic_update_slice.120 = bf16[128,2,1024]{0,2,1:T(8,128)(2,1)S(1)} dynamic-update-slice(bf16[128,2,1024]{0,2,1:T(8,128)(2,1)S(1)} %dynamic_update_slice.119, bf16[8,2,1024]{0,2,1:T(8,128)(2,1)} %copy.225, s32[]{:T(128)S(6)} %select_n.194, s32[]{:T(128)} %constant.169.clone.1, s32[]{:T(128)} %constant.169.clone.1) | dynamic-update-slice | bytes 65540 | tf_op jit(solution)/shard_map/dynamic_update_slice | solution.py:159
  512.3 5.8 %dynamic_update_slice.121 = bf16[128,2,1024]{0,2,1:T(8,128)(2,1)S(1)} dynamic-update-slice(bf16[128,2,1024]{0,2,1:T(8,128)(2,1)S(1)} %dynamic_update_slice.120, bf16[8,2,1024]{0,2,1:T(8,128)(2,1)} %copy.226, s32[]{:T(128)S(6)} %select_n.196, s32[]{:T(128)} %constant.169.clone.1, s32[]{:T(128)} %constant.169.clone.1) | dynamic-update-slice | bytes 65540 | tf_op jit(solution)/shard_map/dynamic_update_slice | solution.py:152
  519.2 5.8 %dynamic_update_slice.122 = bf16[128,2,1024]{0,2,1:T(8,128)(2,1)S(1)} dynamic-update-slice(bf16[128,2,1024]{0,2,1:T(8,128)(2,1)S(1)} %dynamic_update_slice.121, bf16[8,2,1024]{0,2,1:T(8,128)(2,1)} %copy.227, s32[]{:T(128)S(6)} %select_n.198, s32[]{:T(128)} %constant.169.clone.1, s32[]{:T(128)} %constant.169.clone.1) | dynamic-update-slice | bytes 65540 | tf_op jit(solution)/shard_map/dynamic_update_slice | solution.py:159
  526.0 5.8 %dynamic_update_slice.123 = bf16[128,2,1024]{0,2,1:T(8,128)(2,1)S(1)} dynamic-update-slice(bf16[128,2,1024]{0,2,1:T(8,128)(2,1)S(1)} %dynamic_update_slice.122, bf16[8,2,1024]{0,2,1:T(8,128)(2,1)} %copy.228, s32[]{:T(128)S(6)} %select_n.200, s32[]{:T(128)} %constant.169.clone.1, s32[]{:T(128)} %constant.169.clone.1) | dynamic-update-slice | bytes 65540 | tf_op jit(solution)/shard_map/dynamic_update_slice | solution.py:152
  532.9 5.8 %dynamic_update_slice.124 = bf16[128,2,1024]{0,2,1:T(8,128)(2,1)S(1)} dynamic-update-slice(bf16[128,2,1024]{0,2,1:T(8,128)(2,1)S(1)} %dynamic_update_slice.123, bf16[8,2,1024]{0,2,1:T(8,128)(2,1)} %copy.229, s32[]{:T(128)S(6)} %select_n.202, s32[]{:T(128)} %constant.169.clone.1, s32[]{:T(128)} %constant.169.clone.1) | dynamic-update-slice | bytes 65540 | tf_op jit(solution)/shard_map/dynamic_update_slice | solution.py:159
  539.7 6.0 %dynamic_update_slice.125 = bf16[128,2,1024]{0,2,1:T(8,128)(2,1)S(1)} dynamic-update-slice(bf16[128,2,1024]{0,2,1:T(8,128)(2,1)S(1)} %dynamic_update_slice.124, bf16[8,2,1024]{0,2,1:T(8,128)(2,1)} %copy.230, s32[]{:T(128)S(6)} %select_n.204, s32[]{:T(128)} %constant.169.clone.1, s32[]{:T(128)} %constant.169.clone.1) | dynamic-update-slice | bytes 65540 | tf_op jit(solution)/shard_map/dynamic_update_slice | solution.py:152
  546.7 5.8 %dynamic_update_slice.126 = bf16[128,2,1024]{0,2,1:T(8,128)(2,1)S(1)} dynamic-update-slice(bf16[128,2,1024]{0,2,1:T(8,128)(2,1)S(1)} %dynamic_update_slice.125, bf16[8,2,1024]{0,2,1:T(8,128)(2,1)} %copy.231, s32[]{:T(128)S(6)} %select_n.206, s32[]{:T(128)} %constant.169.clone.1, s32[]{:T(128)} %constant.169.clone.1) | dynamic-update-slice | bytes 65540 | tf_op jit(solution)/shard_map/dynamic_update_slice | solution.py:159
  554.4 5.8 %dynamic_update_slice.127 = bf16[128,2,1024]{0,2,1:T(8,128)(2,1)S(1)} dynamic-update-slice(bf16[128,2,1024]{0,2,1:T(8,128)(2,1)S(1)} %dynamic_update_slice.126, bf16[8,2,1024]{0,2,1:T(8,128)(2,1)} %copy.232, s32[]{:T(128)S(6)} %select_n.208, s32[]{:T(128)} %constant.169.clone.1, s32[]{:T(128)} %constant.169.clone.1) | dynamic-update-slice | bytes 65540 | tf_op jit(solution)/shard_map/dynamic_update_slice | solution.py:152
  (299 shorter events, 134.4 us)
Async XLA Ops:
  7.2 137.0 %copy-start = (bf16[1,4,9,2,128,128]{5,4,3,2,1,0:T(8,128)(2,1)S(1)}, bf16[1,4,9,2,128,128]{5,4,3,2,1,0:T(8,128)(2,1)}, u32[]{:S(2)}) copy-start(bf16[1,4,9,2,128,128]{5,4,3,2,1,0:T(8,128)(2,1)} %param.11) | copy-start | bytes 7077892
  7.2 105.1 %reduce-scatter.3.cloned.1.call-start = ((), (), s32[]{:S(2)}) async-start(), calls=%async_computation.2 | async-start | bytes 1114112 | tf_op jit(solution)/shard_map/reduce_scatter | solution.py:132
  44.6 30.9 %copy-start.12 = (bf16[1,4,2,8,128]{4,3,1,2,0:T(8,128)(2,1)}, bf16[1,4,2,8,128]{4,3,1,2,0:T(8,128)(2,1)S(1)}, u32[]{:S(2)}) copy-start(bf16[1,4,2,8,128]{4,3,1,2,0:T(8,128)(2,1)S(1)} %fusion.22) | copy-start | bytes 49156
  44.6 24.0 %collective-permute-start = (bf16[1,4,2,8,128]{4,3,1,2,0:T(8,128)(2,1)S(1)}, bf16[1,4,2,8,128]{4,3,1,2,0:T(8,128)(2,1)}, u32[]{:S(2)}, u32[]{:S(2)}) collective-permute-start(bf16[1,4,2,8,128]{4,3,1,2,0:T(8,128)(2,1)S(1)} %fusion.22), channel_id=1, source_target_pairs={{0,2},{2,4},{4,6},{6,8},{8,10},{10,12},{12,14},{14,0},{1,3},{3,5},... | collective-permute-start | bytes 49160 | tf_op jit(solution)/shard_map/ppermute | solution.py:18
  44.6 24.0 %collective-permute-start.1 = (bf16[1,4,2,8,128]{4,3,1,2,0:T(8,128)(2,1)S(1)}, bf16[1,4,2,8,128]{4,3,1,2,0:T(8,128)(2,1)}, u32[]{:S(2)}, u32[]{:S(2)}) collective-permute-start(bf16[1,4,2,8,128]{4,3,1,2,0:T(8,128)(2,1)S(1)} %fusion.22), channel_id=1, source_target_pairs={{2,0},{4,2},{6,4},{8,6},{10,8},{12,10},{14,12},{0,14},{3,1},{5,3},... | collective-permute-start | bytes 49160 | tf_op jit(solution)/shard_map/ppermute | solution.py:19
  57.4 348.4 %reduce-scatter.5.cloned.1.call-start = ((), (), s32[]{:S(2)}) async-start(), calls=%async_computation.3 | async-start | bytes 1114112 | tf_op jit(solution)/shard_map/reduce_scatter | solution.py:132
  70.0 4.7 collective-permute-start.2
  71.8 59.7 %copy-start.14 = (f32[8,1,1024]{2,0,1:T(8,128)}, f32[8,1,1024]{2,0,1:T(8,128)S(1)}, u32[]{:S(2)}) copy-start(f32[8,1,1024]{2,0,1:T(8,128)S(1)} %copy.178) | copy-start | bytes 98308
  73.4 2.1 collective-permute-start.3
  113.2 6.0 %collective-permute-start.4 = (bf16[8,2,1024]{2,0,1:T(8,128)(2,1)S(1)}, bf16[8,2,1024]{2,0,1:T(8,128)(2,1)S(1)}, u32[]{:S(2)}, u32[]{:S(2)}) collective-permute-start(bf16[8,2,1024]{2,0,1:T(8,128)(2,1)S(1)} %multiply_convert_fusion.1), channel_id=1, source_target_pairs={{0,1},{1,2},{2,3},{3,4},{4,5},{5,6},{6,7},{7,8},{8,9},{9,10},{10,1... | collective-permute-start | bytes 98312 | tf_op jit(solution)/shard_map/ppermute | solution.py:149
  113.2 6.1 %collective-permute-start.5 = (bf16[8,2,1024]{2,0,1:T(8,128)(2,1)S(1)}, bf16[8,2,1024]{2,0,1:T(8,128)(2,1)S(1)}, u32[]{:S(2)}, u32[]{:S(2)}) collective-permute-start(bf16[8,2,1024]{2,0,1:T(8,128)(2,1)S(1)} %multiply_convert_fusion.1), channel_id=1, source_target_pairs={{0,15},{1,0},{2,1},{3,2},{4,3},{5,4},{6,5},{7,6},{8,7},{9,8},{10,9... | collective-permute-start | bytes 98312 | tf_op jit(solution)/shard_map/ppermute | solution.py:156
  119.2 6.1 %collective-permute-start.6 = (bf16[8,2,1024]{2,0,1:T(8,128)(2,1)S(1)}, bf16[8,2,1024]{2,0,1:T(8,128)(2,1)S(1)}, u32[]{:S(2)}, u32[]{:S(2)}) collective-permute-start(bf16[8,2,1024]{2,0,1:T(8,128)(2,1)S(1)} %collective-permute-done.4), channel_id=1, source_target_pairs={{0,1},{1,2},{2,3},{3,4},{4,5},{5,6},{6,7},{7,8},{8,9},{9,10},{10,1... | collective-permute-start | bytes 98312 | tf_op jit(solution)/shard_map/ppermute | solution.py:149
  119.3 6.1 %collective-permute-start.7 = (bf16[8,2,1024]{2,0,1:T(8,128)(2,1)S(1)}, bf16[8,2,1024]{2,0,1:T(8,128)(2,1)S(1)}, u32[]{:S(2)}, u32[]{:S(2)}) collective-permute-start(bf16[8,2,1024]{2,0,1:T(8,128)(2,1)S(1)} %collective-permute-done.5), channel_id=1, source_target_pairs={{0,15},{1,0},{2,1},{3,2},{4,3},{5,4},{6,5},{7,6},{8,7},{9,8},{10,9... | collective-permute-start | bytes 98312 | tf_op jit(solution)/shard_map/ppermute | solution.py:156
  125.3 6.1 %collective-permute-start.8 = (bf16[8,2,1024]{2,0,1:T(8,128)(2,1)S(1)}, bf16[8,2,1024]{2,0,1:T(8,128)(2,1)}, u32[]{:S(2)}, u32[]{:S(2)}) collective-permute-start(bf16[8,2,1024]{2,0,1:T(8,128)(2,1)S(1)} %collective-permute-done.6), channel_id=1, source_target_pairs={{0,1},{1,2},{2,3},{3,4},{4,5},{5,6},{6,7},{7,8},{8,9},{9,10},{10,1... | collective-permute-start | bytes 98312 | tf_op jit(solution)/shard_map/ppermute | solution.py:149
  125.4 7.7 %collective-permute-start.9 = (bf16[8,2,1024]{2,0,1:T(8,128)(2,1)S(1)}, bf16[8,2,1024]{2,0,1:T(8,128)(2,1)S(1)}, u32[]{:S(2)}, u32[]{:S(2)}) collective-permute-start(bf16[8,2,1024]{2,0,1:T(8,128)(2,1)S(1)} %collective-permute-done.7), channel_id=1, source_target_pairs={{0,15},{1,0},{2,1},{3,2},{4,3},{5,4},{6,5},{7,6},{8,7},{9,8},{10,9... | collective-permute-start | bytes 98312 | tf_op jit(solution)/shard_map/ppermute | solution.py:156
  131.5 6.4 %collective-permute-start.10 = (bf16[8,2,1024]{2,0,1:T(8,128)(2,1)}, bf16[8,2,1024]{2,0,1:T(8,128)(2,1)}, u32[]{:S(2)}, u32[]{:S(2)}) collective-permute-start(bf16[8,2,1024]{2,0,1:T(8,128)(2,1)} %collective-permute-done.8), channel_id=1, source_target_pairs={{0,1},{1,2},{2,3},{3,4},{4,5},{5,6},{6,7},{7,8},{8,9},{9,10},{10,1... | collective-permute-start | bytes 98312 | tf_op jit(solution)/shard_map/ppermute | solution.py:149
  133.1 6.1 %collective-permute-start.11 = (bf16[8,2,1024]{2,0,1:T(8,128)(2,1)S(1)}, bf16[8,2,1024]{2,0,1:T(8,128)(2,1)}, u32[]{:S(2)}, u32[]{:S(2)}) collective-permute-start(bf16[8,2,1024]{2,0,1:T(8,128)(2,1)S(1)} %collective-permute-done.9), channel_id=1, source_target_pairs={{0,15},{1,0},{2,1},{3,2},{4,3},{5,4},{6,5},{7,6},{8,7},{9,8},{10,9... | collective-permute-start | bytes 98312 | tf_op jit(solution)/shard_map/ppermute | solution.py:156
  137.8 6.4 %collective-permute-start.12 = (bf16[8,2,1024]{2,0,1:T(8,128)(2,1)}, bf16[8,2,1024]{2,0,1:T(8,128)(2,1)}, u32[]{:S(2)}, u32[]{:S(2)}) collective-permute-start(bf16[8,2,1024]{2,0,1:T(8,128)(2,1)} %collective-permute-done.10), channel_id=1, source_target_pairs={{0,1},{1,2},{2,3},{3,4},{4,5},{5,6},{6,7},{7,8},{8,9},{9,10},{10,1... | collective-permute-start | bytes 98312 | tf_op jit(solution)/shard_map/ppermute | solution.py:149
  139.2 6.5 %collective-permute-start.13 = (bf16[8,2,1024]{2,0,1:T(8,128)(2,1)}, bf16[8,2,1024]{2,0,1:T(8,128)(2,1)S(1)}, u32[]{:S(2)}, u32[]{:S(2)}) collective-permute-start(bf16[8,2,1024]{2,0,1:T(8,128)(2,1)} %collective-permute-done.11), channel_id=1, source_target_pairs={{0,15},{1,0},{2,1},{3,2},{4,3},{5,4},{6,5},{7,6},{8,7},{9,8},{10,9... | collective-permute-start | bytes 98312 | tf_op jit(solution)/shard_map/ppermute | solution.py:156
  144.2 6.3 %collective-permute-start.14 = (bf16[8,2,1024]{2,0,1:T(8,128)(2,1)}, bf16[8,2,1024]{2,0,1:T(8,128)(2,1)S(1)}, u32[]{:S(2)}, u32[]{:S(2)}) collective-permute-start(bf16[8,2,1024]{2,0,1:T(8,128)(2,1)} %collective-permute-done.12), channel_id=1, source_target_pairs={{0,1},{1,2},{2,3},{3,4},{4,5},{5,6},{6,7},{7,8},{8,9},{9,10},{10,1... | collective-permute-start | bytes 98312 | tf_op jit(solution)/shard_map/ppermute | solution.py:149
  145.6 5.9 %collective-permute-start.15 = (bf16[8,2,1024]{2,0,1:T(8,128)(2,1)S(1)}, bf16[8,2,1024]{2,0,1:T(8,128)(2,1)S(1)}, u32[]{:S(2)}, u32[]{:S(2)}) collective-permute-start(bf16[8,2,1024]{2,0,1:T(8,128)(2,1)S(1)} %collective-permute-done.13), channel_id=1, source_target_pairs={{0,15},{1,0},{2,1},{3,2},{4,3},{5,4},{6,5},{7,6},{8,7},{9,8},{10,9... | collective-permute-start | bytes 98312 | tf_op jit(solution)/shard_map/ppermute | solution.py:156
  150.5 6.1 %collective-permute-start.16 = (bf16[8,2,1024]{2,0,1:T(8,128)(2,1)S(1)}, bf16[8,2,1024]{2,0,1:T(8,128)(2,1)}, u32[]{:S(2)}, u32[]{:S(2)}) collective-permute-start(bf16[8,2,1024]{2,0,1:T(8,128)(2,1)S(1)} %collective-permute-done.14), channel_id=1, source_target_pairs={{0,1},{1,2},{2,3},{3,4},{4,5},{5,6},{6,7},{7,8},{8,9},{9,10},{10,1... | collective-permute-start | bytes 98312 | tf_op jit(solution)/shard_map/ppermute | solution.py:149
  151.6 104.8 %collective-permute-start.17 = (bf16[8,2,1024]{2,0,1:T(8,128)(2,1)S(1)}, bf16[8,2,1024]{2,0,1:T(8,128)(2,1)}, u32[]{:S(2)}, u32[]{:S(2)}) collective-permute-start(bf16[8,2,1024]{2,0,1:T(8,128)(2,1)S(1)} %collective-permute-done.15), channel_id=1, source_target_pairs={{0,15},{1,0},{2,1},{3,2},{4,3},{5,4},{6,5},{7,6},{8,7},{9,8},{10,9... | collective-permute-start | bytes 98312 | tf_op jit(solution)/shard_map/ppermute | solution.py:156
  156.6 107.4 %collective-permute-start.18 = (bf16[8,2,1024]{2,0,1:T(8,128)(2,1)}, bf16[8,2,1024]{2,0,1:T(8,128)(2,1)}, u32[]{:S(2)}, u32[]{:S(2)}) collective-permute-start(bf16[8,2,1024]{2,0,1:T(8,128)(2,1)} %collective-permute-done.16), channel_id=1, source_target_pairs={{0,1},{1,2},{2,3},{3,4},{4,5},{5,6},{6,7},{7,8},{8,9},{9,10},{10,1... | collective-permute-start | bytes 98312 | tf_op jit(solution)/shard_map/ppermute | solution.py:149
  206.9 21.1 %copy-start.21 = (bf16[8,2,1024]{2,0,1:T(8,128)(2,1)S(1)}, bf16[8,2,1024]{2,0,1:T(8,128)(2,1)}, u32[]{:S(2)}) copy-start(bf16[8,2,1024]{2,0,1:T(8,128)(2,1)} %copy-done.20) | copy-start | bytes 98308
  214.6 20.3 %copy-start.23 = (bf16[8,2,1024]{2,0,1:T(8,128)(2,1)S(1)}, bf16[8,2,1024]{2,0,1:T(8,128)(2,1)}, u32[]{:S(2)}) copy-start(bf16[8,2,1024]{2,0,1:T(8,128)(2,1)} %copy-done.22) | copy-start | bytes 98308
  273.6 73.9 %copy-start.2 = (f32[512,128]{0,1:T(8,128)S(1)}, f32[512,128]{0,1:T(8,128)}, u32[]{:S(2)}) copy-start(f32[512,128]{0,1:T(8,128)} %copy-done.1) | copy-start | bytes 786436
  342.7 8.4 %collective-permute-start.19 = (bf16[1,4,2,8,128]{4,3,1,2,0:T(8,128)(2,1)S(1)}, bf16[1,4,2,8,128]{4,3,1,2,0:T(8,128)(2,1)S(1)}, u32[]{:S(2)}, u32[]{:S(2)}) collective-permute-start(bf16[1,4,2,8,128]{4,3,1,2,0:T(8,128)(2,1)S(1)} %fusion.20), channel_id=1, source_target_pairs={{0,2},{2,4},{4,6},{6,8},{8,10},{10,12},{12,14},{14,0},{1,3},{3,5},... | collective-permute-start | bytes 49160 | tf_op jit(solution)/shard_map/ppermute | solution.py:18
  342.7 8.4 %collective-permute-start.20 = (bf16[1,4,2,8,128]{4,3,1,2,0:T(8,128)(2,1)S(1)}, bf16[1,4,2,8,128]{4,3,1,2,0:T(8,128)(2,1)S(1)}, u32[]{:S(2)}, u32[]{:S(2)}) collective-permute-start(bf16[1,4,2,8,128]{4,3,1,2,0:T(8,128)(2,1)S(1)} %fusion.20), channel_id=1, source_target_pairs={{2,0},{4,2},{6,4},{8,6},{10,8},{12,10},{14,12},{0,14},{3,1},{5,3},... | collective-permute-start | bytes 49160 | tf_op jit(solution)/shard_map/ppermute | solution.py:19
  349.9 55.9 %copy-start.15 = (f32[8,1,1024]{2,0,1:T(8,128)S(1)}, f32[8,1,1024]{2,0,1:T(8,128)}, u32[]{:S(2)}) copy-start(f32[8,1,1024]{2,0,1:T(8,128)} %copy-done.14) | copy-start | bytes 98308
  351.1 79.9 %copy-start.26 = (pred[4,9]{1,0:T(4,128)(4,1)S(1)}, pred[4,9]{1,0:T(4,128)(4,1)}, u32[]{:S(2)}) copy-start(pred[4,9]{1,0:T(4,128)(4,1)} %and_bitcast_fusion) | copy-start | bytes 112
  351.1 1.2 collective-permute-start.22
  351.8 1.3 collective-permute-start.21
  406.6 6.0 %collective-permute-start.23 = (bf16[8,2,1024]{2,0,1:T(8,128)(2,1)S(1)}, bf16[8,2,1024]{2,0,1:T(8,128)(2,1)S(1)}, u32[]{:S(2)}, u32[]{:S(2)}) collective-permute-start(bf16[8,2,1024]{2,0,1:T(8,128)(2,1)S(1)} %multiply_convert_fusion), channel_id=1, source_target_pairs={{0,1},{1,2},{2,3},{3,4},{4,5},{5,6},{6,7},{7,8},{8,9},{9,10},{10,1... | collective-permute-start | bytes 98312 | tf_op jit(solution)/shard_map/ppermute | solution.py:149
  406.7 6.1 %collective-permute-start.24 = (bf16[8,2,1024]{2,0,1:T(8,128)(2,1)S(1)}, bf16[8,2,1024]{2,0,1:T(8,128)(2,1)S(1)}, u32[]{:S(2)}, u32[]{:S(2)}) collective-permute-start(bf16[8,2,1024]{2,0,1:T(8,128)(2,1)S(1)} %multiply_convert_fusion), channel_id=1, source_target_pairs={{0,15},{1,0},{2,1},{3,2},{4,3},{5,4},{6,5},{7,6},{8,7},{9,8},{10,9... | collective-permute-start | bytes 98312 | tf_op jit(solution)/shard_map/ppermute | solution.py:156
  412.7 6.1 %collective-permute-start.25 = (bf16[8,2,1024]{2,0,1:T(8,128)(2,1)S(1)}, bf16[8,2,1024]{2,0,1:T(8,128)(2,1)S(1)}, u32[]{:S(2)}, u32[]{:S(2)}) collective-permute-start(bf16[8,2,1024]{2,0,1:T(8,128)(2,1)S(1)} %collective-permute-done.23), channel_id=1, source_target_pairs={{0,1},{1,2},{2,3},{3,4},{4,5},{5,6},{6,7},{7,8},{8,9},{9,10},{10,1... | collective-permute-start | bytes 98312 | tf_op jit(solution)/shard_map/ppermute | solution.py:149
  412.8 6.1 %collective-permute-start.26 = (bf16[8,2,1024]{2,0,1:T(8,128)(2,1)S(1)}, bf16[8,2,1024]{2,0,1:T(8,128)(2,1)S(1)}, u32[]{:S(2)}, u32[]{:S(2)}) collective-permute-start(bf16[8,2,1024]{2,0,1:T(8,128)(2,1)S(1)} %collective-permute-done.24), channel_id=1, source_target_pairs={{0,15},{1,0},{2,1},{3,2},{4,3},{5,4},{6,5},{7,6},{8,7},{9,8},{10,9... | collective-permute-start | bytes 98312 | tf_op jit(solution)/shard_map/ppermute | solution.py:156
  418.8 6.0 %collective-permute-start.27 = (bf16[8,2,1024]{2,0,1:T(8,128)(2,1)S(1)}, bf16[8,2,1024]{2,0,1:T(8,128)(2,1)S(1)}, u32[]{:S(2)}, u32[]{:S(2)}) collective-permute-start(bf16[8,2,1024]{2,0,1:T(8,128)(2,1)S(1)} %collective-permute-done.25), channel_id=1, source_target_pairs={{0,1},{1,2},{2,3},{3,4},{4,5},{5,6},{6,7},{7,8},{8,9},{9,10},{10,1... | collective-permute-start | bytes 98312 | tf_op jit(solution)/shard_map/ppermute | solution.py:149
  418.9 7.6 %collective-permute-start.28 = (bf16[8,2,1024]{2,0,1:T(8,128)(2,1)S(1)}, bf16[8,2,1024]{2,0,1:T(8,128)(2,1)S(1)}, u32[]{:S(2)}, u32[]{:S(2)}) collective-permute-start(bf16[8,2,1024]{2,0,1:T(8,128)(2,1)S(1)} %collective-permute-done.26), channel_id=1, source_target_pairs={{0,15},{1,0},{2,1},{3,2},{4,3},{5,4},{6,5},{7,6},{8,7},{9,8},{10,9... | collective-permute-start | bytes 98312 | tf_op jit(solution)/shard_map/ppermute | solution.py:156
  424.9 6.1 %collective-permute-start.29 = (bf16[8,2,1024]{2,0,1:T(8,128)(2,1)S(1)}, bf16[8,2,1024]{2,0,1:T(8,128)(2,1)S(1)}, u32[]{:S(2)}, u32[]{:S(2)}) collective-permute-start(bf16[8,2,1024]{2,0,1:T(8,128)(2,1)S(1)} %collective-permute-done.27), channel_id=1, source_target_pairs={{0,1},{1,2},{2,3},{3,4},{4,5},{5,6},{6,7},{7,8},{8,9},{9,10},{10,1... | collective-permute-start | bytes 98312 | tf_op jit(solution)/shard_map/ppermute | solution.py:149
  426.4 6.1 %collective-permute-start.30 = (bf16[8,2,1024]{2,0,1:T(8,128)(2,1)S(1)}, bf16[8,2,1024]{2,0,1:T(8,128)(2,1)S(1)}, u32[]{:S(2)}, u32[]{:S(2)}) collective-permute-start(bf16[8,2,1024]{2,0,1:T(8,128)(2,1)S(1)} %collective-permute-done.28), channel_id=1, source_target_pairs={{0,15},{1,0},{2,1},{3,2},{4,3},{5,4},{6,5},{7,6},{8,7},{9,8},{10,9... | collective-permute-start | bytes 98312 | tf_op jit(solution)/shard_map/ppermute | solution.py:156
  430.9 6.1 %collective-permute-start.31 = (bf16[8,2,1024]{2,0,1:T(8,128)(2,1)S(1)}, bf16[8,2,1024]{2,0,1:T(8,128)(2,1)}, u32[]{:S(2)}, u32[]{:S(2)}) collective-permute-start(bf16[8,2,1024]{2,0,1:T(8,128)(2,1)S(1)} %collective-permute-done.29), channel_id=1, source_target_pairs={{0,1},{1,2},{2,3},{3,4},{4,5},{5,6},{6,7},{7,8},{8,9},{9,10},{10,1... | collective-permute-start | bytes 98312 | tf_op jit(solution)/shard_map/ppermute | solution.py:149
  432.5 6.0 %collective-permute-start.32 = (bf16[8,2,1024]{2,0,1:T(8,128)(2,1)S(1)}, bf16[8,2,1024]{2,0,1:T(8,128)(2,1)S(1)}, u32[]{:S(2)}, u32[]{:S(2)}) collective-permute-start(bf16[8,2,1024]{2,0,1:T(8,128)(2,1)S(1)} %collective-permute-done.30), channel_id=1, source_target_pairs={{0,15},{1,0},{2,1},{3,2},{4,3},{5,4},{6,5},{7,6},{8,7},{9,8},{10,9... | collective-permute-start | bytes 98312 | tf_op jit(solution)/shard_map/ppermute | solution.py:156
  437.1 6.3 %collective-permute-start.33 = (bf16[8,2,1024]{2,0,1:T(8,128)(2,1)}, bf16[8,2,1024]{2,0,1:T(8,128)(2,1)S(1)}, u32[]{:S(2)}, u32[]{:S(2)}) collective-permute-start(bf16[8,2,1024]{2,0,1:T(8,128)(2,1)} %collective-permute-done.31), channel_id=1, source_target_pairs={{0,1},{1,2},{2,3},{3,4},{4,5},{5,6},{6,7},{7,8},{8,9},{9,10},{10,1... | collective-permute-start | bytes 98312 | tf_op jit(solution)/shard_map/ppermute | solution.py:149
  438.6 6.0 %collective-permute-start.34 = (bf16[8,2,1024]{2,0,1:T(8,128)(2,1)S(1)}, bf16[8,2,1024]{2,0,1:T(8,128)(2,1)S(1)}, u32[]{:S(2)}, u32[]{:S(2)}) collective-permute-start(bf16[8,2,1024]{2,0,1:T(8,128)(2,1)S(1)} %collective-permute-done.32), channel_id=1, source_target_pairs={{0,15},{1,0},{2,1},{3,2},{4,3},{5,4},{6,5},{7,6},{8,7},{9,8},{10,9... | collective-permute-start | bytes 98312 | tf_op jit(solution)/shard_map/ppermute | solution.py:156
  443.4 6.0 %collective-permute-start.35 = (bf16[8,2,1024]{2,0,1:T(8,128)(2,1)S(1)}, bf16[8,2,1024]{2,0,1:T(8,128)(2,1)S(1)}, u32[]{:S(2)}, u32[]{:S(2)}) collective-permute-start(bf16[8,2,1024]{2,0,1:T(8,128)(2,1)S(1)} %collective-permute-done.33), channel_id=1, source_target_pairs={{0,1},{1,2},{2,3},{3,4},{4,5},{5,6},{6,7},{7,8},{8,9},{9,10},{10,1... | collective-permute-start | bytes 98312 | tf_op jit(solution)/shard_map/ppermute | solution.py:149
  444.6 101.1 %collective-permute-start.36 = (bf16[8,2,1024]{2,0,1:T(8,128)(2,1)S(1)}, bf16[8,2,1024]{2,0,1:T(8,128)(2,1)S(1)}, u32[]{:S(2)}, u32[]{:S(2)}) collective-permute-start(bf16[8,2,1024]{2,0,1:T(8,128)(2,1)S(1)} %collective-permute-done.34), channel_id=1, source_target_pairs={{0,15},{1,0},{2,1},{3,2},{4,3},{5,4},{6,5},{7,6},{8,7},{9,8},{10,9... | collective-permute-start | bytes 98312 | tf_op jit(solution)/shard_map/ppermute | solution.py:156
  449.4 103.2 %collective-permute-start.37 = (bf16[8,2,1024]{2,0,1:T(8,128)(2,1)S(1)}, bf16[8,2,1024]{2,0,1:T(8,128)(2,1)}, u32[]{:S(2)}, u32[]{:S(2)}) collective-permute-start(bf16[8,2,1024]{2,0,1:T(8,128)(2,1)S(1)} %collective-permute-done.35), channel_id=1, source_target_pairs={{0,1},{1,2},{2,3},{3,4},{4,5},{5,6},{6,7},{7,8},{8,9},{9,10},{10,1... | collective-permute-start | bytes 98312 | tf_op jit(solution)/shard_map/ppermute | solution.py:149
  (20 other events, 132.1 us)
Sparse Core Ops, SparseCore 0:
  57.6 54.7 reduce-scatter.2
  351.2 54.5 reduce-scatter.4
